TPU v7x, 32 devices: a whole 2x2x4 slice. The times are simulated.
32 devices in a mesh: dp: 4 (over y, core), expert: 2 (over x), tensor: 4 (over z).
Axes of the slice: x: 2, y: 2, z: 4, core: 2. Of those that a mesh axis runs over, the one named last changes fastest.
Arguments:
- inputs: bfloat16 [1576, 768], P(('dp', 'expert')), may hold values from -6 to 6
- first_gain: float32 [768], replicated, may hold values from 0.5 to 1.5
- first_bias: float32 [768], replicated, may hold values from -2 to 2
- attention_in: bfloat16 [3, 768, 768], P(None, None, 'tensor')
- attention_out: bfloat16 [768, 768], P('tensor'), may hold values from -0.875 to 0.875
- second_gain: float32 [768], replicated, may hold values from 0.5 to 1.5
- second_bias: float32 [768], replicated, may hold values from -2 to 2
- router_weight: float32 [768, 4], replicated
- expert_in: bfloat16 [4, 768, 3072], P('expert', None, 'tensor'), may hold values from -0.21875 to 0.21875
- expert_out: bfloat16 [4, 3072, 768], P('expert', 'tensor'), may hold values from -1.75 to 1.75
- expert_ids: int32 [1576, 2], P(('dp', 'expert')), may hold values from 0 to 3, as said below
- slot_index: int32 [1576, 2], P(('dp', 'expert')), may hold values from 0 to 98, as said below
- cotangent: bfloat16 [1576, 768], P(('dp', 'expert')), may hold values from -6 to 6
Outputs:
- layer_out: float32 [1576, 768], P(('dp', 'expert'))
- input_grad: float32 [1576, 768], P(('dp', 'expert'))
- first_gain_grad: float32 [768], P(('dp', 'expert'))
- first_bias_grad: float32 [768], P(('dp', 'expert'))
- attention_in_grad: float32 [3, 768, 768], P(None, ('dp', 'expert'), 'tensor')
- attention_out_grad: float32 [768, 768], P('tensor', ('dp', 'expert'))
- second_gain_grad: float32 [768], P(('dp', 'expert'))
- second_bias_grad: float32 [768], P(('dp', 'expert'))
- router_grad: float32 [768, 4], P(('dp', 'expert'))
- expert_in_grad: float32 [4, 768, 3072], P('expert', 'dp', 'tensor')
- expert_out_grad: float32 [4, 3072, 768], P('expert', 'tensor', 'dp')
Inputs may be any that keep to these rules, and one draw needn't show every extreme that they name: `expert_ids`: the two experts of a token differ. `slot_index`: among the 197 tokens of one index of dp and expert, the choices naming one expert hold slots 0, 1, 2 and so on, all first choices before all second choices, rows in order within each; a choice ranked 98 or later holds 98 and is dropped. Some expert fills all 98 slots from every index of dp and expert.
All inputs are finite; a program needn't handle non-finite values.
Results may differ from a plain program's by a relative error of at most 0.02.
Values may be sent and summed in bfloat16 or wider, within the bound.
A program may use at most 128 MiB of HBM per device.

v0:
```python
import math
import jax
import jax.numpy as jnp
from jax import lax
from jax.sharding import PartitionSpec as P

HEAD_DIM = 64
SEQ = 197
EPS = 1e-06
GELU_C = math.sqrt(2.0 / math.pi)


def cut_along(shard, dim, devices):
    shape = shard.shape
    tiles = shard.reshape(*shape[:dim], devices, shape[dim] // devices, *shape[dim + 1 :])
    return jnp.moveaxis(tiles, dim, 0)


def sent_and_summed(shard, axis, dim):
    devices = lax.axis_size(axis)
    tiles = lax.all_to_all(cut_along(shard, dim, devices), axis, 0, 0, tiled=True)
    return jnp.sum(tiles.astype(jnp.float32), axis=0)


def sent_together(arrays, axis, dim, along):
    widths = [math.prod(a.shape[along:]) for a in arrays]
    both = jnp.concatenate(
        [a.reshape(*a.shape[:along], w) for a, w in zip(arrays, widths)], axis=along
    )
    out = sent_and_summed(both, axis, dim)
    tiles = jnp.split(out, [sum(widths[:k]) for k in range(1, len(widths))], axis=along)
    return tuple((b.reshape(*out.shape[:along], *a.shape[along:]) for a, b in zip(arrays, tiles)))


def normalize(values):
    centre = jnp.mean(values, axis=-1, keepdims=True)
    centred = values - centre
    spread = jnp.mean(centred * centred, axis=-1, keepdims=True)
    scale = lax.rsqrt(spread + EPS)
    return (centred * scale, scale)


def norm_back(grad_out, normed, scale, gain):
    scaled = grad_out * gain
    first_mean = jnp.mean(scaled, axis=-1, keepdims=True)
    second_mean = jnp.mean(scaled * normed, axis=-1, keepdims=True)
    return scale * (scaled - first_mean - normed * second_mean)


def gelu_parts(pre):
    inner = GELU_C * (pre + 0.044715 * pre * pre * pre)
    tangent = jnp.tanh(inner)
    value = 0.5 * pre * (1.0 + tangent)
    slope = 0.5 * (1.0 + tangent) + 0.5 * pre * (1.0 - tangent * tangent) * GELU_C * (
        1.0 + 3.0 * 0.044715 * pre * pre
    )
    return (value, slope)


def per_device(
    inputs,
    first_gain,
    first_bias,
    attention_in,
    attention_out,
    second_gain,
    second_bias,
    router_weight,
    expert_in,
    expert_out,
    expert_ids,
    slot_index,
    cotangent,
):
    tokens_here = inputs.shape[0]
    model_width = inputs.shape[1]
    images = tokens_here // SEQ
    local_width = attention_in.shape[2]
    local_heads = local_width // HEAD_DIM
    owners = lax.axis_size("expert")
    experts_here = expert_in.shape[0]
    experts_all = experts_here * owners
    capacity = (2 * tokens_here - 1) // experts_all
    scaling = HEAD_DIM ** (-0.5)

    def split_heads(matrix):
        return matrix.reshape(images, SEQ, local_heads, HEAD_DIM)

    x_full = inputs.astype(jnp.float32)
    normed1, scale1 = normalize(x_full)
    first = (normed1 * first_gain + first_bias).astype(jnp.bfloat16)
    project = [
        jnp.dot(first, attention_in[which], preferred_element_type=jnp.float32).astype(jnp.bfloat16)
        for which in range(3)
    ]
    query_h, keys_h, values_h = [split_heads(part) for part in project]
    scores = (
        jnp.einsum("iqhd,ikhd->ihqk", query_h, keys_h, preferred_element_type=jnp.float32) * scaling
    )
    peak = jnp.max(scores, axis=-1, keepdims=True)
    logsum = peak[..., 0] + jnp.log(jnp.sum(jnp.exp(scores - peak), axis=-1))
    weights = jnp.exp(scores - logsum[..., None]).astype(jnp.bfloat16)
    context_h = jnp.einsum(
        "ihqk,ikhd->iqhd", weights, values_h, preferred_element_type=jnp.float32
    ).astype(jnp.bfloat16)
    context = context_h.reshape(tokens_here, local_width)
    partial_attn = jnp.dot(context, attention_out, preferred_element_type=jnp.float32)
    attended = lax.psum(partial_attn, "tensor")
    resid = x_full + attended
    normed2, scale2 = normalize(resid)
    second = (normed2 * second_gain + second_bias).astype(jnp.bfloat16)
    logits = jnp.dot(second.astype(jnp.float32), router_weight, precision=lax.Precision.HIGHEST)
    route = jax.nn.softmax(logits, axis=-1)
    valid = (slot_index < capacity).astype(jnp.float32)
    choose = (expert_ids[:, :, None] == jnp.arange(experts_all, dtype=jnp.int32)).astype(
        jnp.float32
    )
    gate = jnp.sum(route[:, None, :] * choose, axis=-1) * valid
    target = jnp.where(slot_index < capacity, expert_ids * capacity + slot_index, -1)
    chosen = (target[:, :, None] == jnp.arange(experts_all * capacity, dtype=jnp.int32)).astype(
        jnp.bfloat16
    )
    placing = jnp.sum(chosen, axis=1)
    sendbuf = jnp.einsum("rq,rd->qd", placing, second, preferred_element_type=jnp.float32).astype(
        jnp.bfloat16
    )
    sendbuf = sendbuf.reshape(owners, experts_here, capacity, model_width)
    received = lax.all_to_all(sendbuf, "expert", split_axis=0, concat_axis=0, tiled=True)
    pre = jnp.einsum("skcd,kdf->skcf", received, expert_in, preferred_element_type=jnp.float32)
    value, slope = gelu_parts(pre)
    hidden = value.astype(jnp.bfloat16)
    partial_value = jnp.einsum(
        "skcf,kfd->skcd", hidden, expert_out, preferred_element_type=jnp.float32
    )
    summed = lax.psum(partial_value, "tensor")
    returned = lax.all_to_all(
        summed.astype(jnp.bfloat16), "expert", split_axis=0, concat_axis=0, tiled=True
    )
    outcome = (returned, received, hidden, slope)
    returned = outcome[0]
    received = outcome[1]
    outputs_flat = returned.reshape(experts_all * capacity, model_width)
    picked = jnp.einsum("rjq,qd->rjd", chosen, outputs_flat, preferred_element_type=jnp.float32)
    layer_out = resid + jnp.sum(gate[..., None] * picked, axis=1)
    grad_out = cotangent.astype(jnp.float32)
    gate_grad = jnp.sum(grad_out[:, None, :] * picked, axis=-1) * valid
    slot_gate = jnp.einsum(
        "rjq,rj->q", chosen.astype(jnp.float32), gate, precision=lax.Precision.HIGHEST
    )
    slotted = jnp.einsum("rq,rd->qd", placing, cotangent, preferred_element_type=jnp.float32)
    grad_send = (
        (slot_gate[:, None] * slotted)
        .astype(jnp.bfloat16)
        .reshape(owners, experts_here, capacity, model_width)
    )
    grad_recv = lax.all_to_all(grad_send, "expert", split_axis=0, concat_axis=0, tiled=True)
    hidden = outcome[2]
    slope = outcome[3]
    hidden_grad = jnp.einsum(
        "skcd,kfd->skcf", grad_recv, expert_out, preferred_element_type=jnp.float32
    )
    pre_grad = (hidden_grad * slope).astype(jnp.bfloat16)
    local_out_grad = jnp.einsum(
        "skcf,skcd->kfd", hidden, grad_recv, preferred_element_type=jnp.float32
    )
    local_in_grad = jnp.einsum(
        "skcd,skcf->kdf", received, pre_grad, preferred_element_type=jnp.float32
    )
    partial_back = jnp.einsum(
        "skcf,kdf->skcd", pre_grad, expert_in, preferred_element_type=jnp.float32
    )
    back_sum = lax.psum(partial_back.astype(jnp.bfloat16), "tensor")
    back_home = lax.all_to_all(back_sum, "expert", split_axis=0, concat_axis=0, tiled=True)
    back_rows = jnp.einsum(
        "rjq,qd->rd",
        chosen,
        back_home.reshape(experts_all * capacity, model_width),
        preferred_element_type=jnp.float32,
    )
    expert_in_grad, expert_out_grad = (
        lax.psum_scatter(
            local_in_grad.astype(jnp.bfloat16), "dp", scatter_dimension=1, tiled=True
        ).astype(jnp.float32),
        lax.psum_scatter(
            local_out_grad.astype(jnp.bfloat16), "dp", scatter_dimension=2, tiled=True
        ).astype(jnp.float32),
    )
    route_grad = jnp.sum(gate_grad[:, :, None] * choose, axis=1)
    logit_grad = route * (route_grad - jnp.sum(route * route_grad, axis=-1, keepdims=True))
    local_router = jnp.dot(
        second.astype(jnp.float32).T, logit_grad, precision=lax.Precision.HIGHEST
    )
    second_grad = back_rows + jnp.dot(logit_grad, router_weight.T, precision=lax.Precision.HIGHEST)
    local_second_gain = jnp.sum(second_grad * normed2, axis=0)
    local_second_bias = jnp.sum(second_grad, axis=0)
    resid_grad = grad_out + norm_back(second_grad, normed2, scale2, second_gain)
    resid_low = resid_grad.astype(jnp.bfloat16)
    local_attn_out = jnp.einsum("rh,rd->hd", context, resid_low, preferred_element_type=jnp.float32)
    context_grad = jnp.einsum(
        "rd,hd->rh", resid_low, attention_out, preferred_element_type=jnp.float32
    ).astype(jnp.bfloat16)
    context_g = split_heads(context_grad)
    probs = jnp.exp(scores - logsum[..., None])
    values_grad = jnp.einsum(
        "ihqk,iqhd->ikhd", weights, context_g, preferred_element_type=jnp.float32
    ).astype(jnp.bfloat16)
    probs_grad = jnp.einsum(
        "iqhd,ikhd->ihqk", context_g, values_h, preferred_element_type=jnp.float32
    )
    delta = jnp.transpose(
        jnp.sum(context_g.astype(jnp.float32) * context_h.astype(jnp.float32), axis=-1), (0, 2, 1)
    )
    score_grad = (probs * (probs_grad - delta[..., None]) * scaling).astype(jnp.bfloat16)
    query_grad = jnp.einsum(
        "ihqk,ikhd->iqhd", score_grad, keys_h, preferred_element_type=jnp.float32
    ).astype(jnp.bfloat16)
    keys_grad = jnp.einsum(
        "ihqk,iqhd->ikhd", score_grad, query_h, preferred_element_type=jnp.float32
    ).astype(jnp.bfloat16)
    grads_flat = [
        part.reshape(tokens_here, local_width) for part in (query_grad, keys_grad, values_grad)
    ]
    local_attn_in = jnp.stack(
        [
            jnp.einsum("rd,rh->dh", first, part, preferred_element_type=jnp.float32)
            for part in grads_flat
        ]
    )
    partial_first = jnp.einsum(
        "rh,dh->rd", grads_flat[0], attention_in[0], preferred_element_type=jnp.float32
    )
    partial_first = partial_first + jnp.einsum(
        "rh,dh->rd", grads_flat[1], attention_in[1], preferred_element_type=jnp.float32
    )
    partial_first = partial_first + jnp.einsum(
        "rh,dh->rd", grads_flat[2], attention_in[2], preferred_element_type=jnp.float32
    )
    first_grad = lax.psum(partial_first.astype(jnp.bfloat16), "tensor").astype(jnp.float32)
    local_first_gain = jnp.sum(first_grad * normed1, axis=0)
    local_first_bias = jnp.sum(first_grad, axis=0)
    input_grad = resid_grad + norm_back(first_grad, normed1, scale1, first_gain)
    summed_shared = (
        sent_and_summed(local_attn_in.astype(jnp.bfloat16), ("dp", "expert"), 1),
        sent_and_summed(local_attn_out.astype(jnp.bfloat16), ("dp", "expert"), 1),
        *sent_together(
            (
                local_router.astype(jnp.bfloat16),
                local_first_gain.astype(jnp.bfloat16),
                local_first_bias.astype(jnp.bfloat16),
                local_second_gain.astype(jnp.bfloat16),
                local_second_bias.astype(jnp.bfloat16),
            ),
            ("dp", "expert"),
            0,
            1,
        ),
    )
    (
        attention_in_grad,
        attention_out_grad,
        router_grad,
        first_gain_grad,
        first_bias_grad,
        second_gain_grad,
        second_bias_grad,
    ) = summed_shared
    return (
        layer_out,
        input_grad,
        first_gain_grad,
        first_bias_grad,
        attention_in_grad,
        attention_out_grad,
        second_gain_grad,
        second_bias_grad,
        router_grad,
        expert_in_grad,
        expert_out_grad,
    )


def solution(mesh):
    in_specs = (
        P(("dp", "expert"), None),
        P(),
        P(),
        P(None, None, "tensor"),
        P("tensor", None),
        P(),
        P(),
        P(),
        P("expert", None, "tensor"),
        P("expert", "tensor", None),
        P(("dp", "expert"), None),
        P(("dp", "expert"), None),
        P(("dp", "expert"), None),
    )
    out_specs = (
        P(("dp", "expert"), None),
        P(("dp", "expert"), None),
        P(("dp", "expert")),
        P(("dp", "expert")),
        P(None, ("dp", "expert"), "tensor"),
        P("tensor", ("dp", "expert")),
        P(("dp", "expert")),
        P(("dp", "expert")),
        P(("dp", "expert"), None),
        P("expert", "dp", "tensor"),
        P("expert", "tensor", "dp"),
    )
    return jax.shard_map(
        per_device, mesh=mesh, in_specs=in_specs, out_specs=out_specs, check_vma=False
    )
```

profile of v0, /device:TPU:0, one launch (start us, length us, event | category | flops | bytes accessed | tf_op | source)
XLA Modules:
  0.0 338.7 jit_solution(17743377087618630051)
XLA Ops:
  9.8 1.5 convolution_convert_fusion.12
  15.5 42.5 %all-reduce.5.cloned.1.call-done = f32[197,768]{1,0:T(8,128)} async-done(((f32[197,768]{1,0:T(8,128)}), f32[197,768]{1,0:T(8,128)}) %all-reduce.5.cloned.1.call-update) | async-done | bytes 605200 | tf_op jit(solution)/shard_map/psum | solution.py:108
  61.5 2.1 reshape.284
  63.6 2.4 copy.130
  66.0 4.2 %all-to-all-start = ((bf16[2,2,98,768]{3,1,2,0:T(2,128)(2,1)}), bf16[2,2,98,768]{3,1,2,0:T(2,128)(2,1)}, u32[]{:S(2)}, u32[]{:S(2)}) async-start(bf16[2,2,98,768]{3,1,2,0:T(2,128)(2,1)} %copy.130), calls=%async_computation | async-start | bytes 1204224 | tf_op jit(solution)/shard_map/all_to_all | solution.py:128
  70.7 2.1 fusion.23
  72.8 2.1 reshape.286
  74.9 2.4 copy.134
  77.2 1.5 all-to-all-done
  78.8 4.3 %all-to-all-start.2 = ((bf16[2,2,98,768]{3,1,2,0:T(2,128)(2,1)}), bf16[2,2,98,768]{3,1,2,0:T(2,128)(2,1)}, u32[]{:S(2)}, u32[]{:S(2)}) async-start(bf16[2,2,98,768]{3,1,2,0:T(2,128)(2,1)} %copy.134), calls=%async_computation.2 | async-start | bytes 1204224 | tf_op jit(solution)/shard_map/all_to_all | solution.py:156
  83.1 2.5 fusion.14
  87.5 1.9 copy.177
  89.5 47.3 %all-reduce.10 = bf16[2,2,98,768]{3,1,2,0:T(2,128)(2,1)} all-reduce(f32[2,2,98,768]{3,1,2,0:T(2,128)} %bitcast.163), channel_id=1, replica_groups=mesh['dp'=4,'expert'=2,'tensor'=4] {'tensor'}, use_global_device_ids=true, to_apply=%region_11.12 | all-reduce | flops 301056 | bytes 1806336 | tf_op jit(solution)/shard_map/psum | solution.py:135
  136.7 4.3 %all-to-all-start.1 = ((bf16[2,2,98,768]{3,1,2,0:T(2,128)(2,1)}), bf16[2,2,98,768]{3,1,2,0:T(2,128)(2,1)}, u32[]{:S(2)}, u32[]{:S(2)}) async-start(bf16[2,2,98,768]{3,1,2,0:T(2,128)(2,1)} %all-reduce.10), calls=%async_computation.1 | async-start | bytes 1204224 | tf_op jit(solution)/shard_map/all_to_all | solution.py:136
  141.1 2.9 fusion.17
  144.8 1.7 fusion.29
  146.5 1.8 convert_element_type.218
  148.4 2.0 copy.133
  150.3 2.1 reshape.301
  152.4 2.8 multiply_reduce_fusion
  155.3 31.0 %all-reduce.7.cloned.1.call-done = bf16[2,2,98,768]{3,2,0,1:T(8,128)(2,1)} async-done(((bf16[2,2,98,768]{3,2,0,1:T(8,128)(2,1)}), bf16[2,2,98,768]{3,2,0,1:T(8,128)(2,1)}) %all-reduce.7.cloned.1.call-update) | async-done | bytes 602128 | tf_op jit(solution)/shard_map/psum | solution.py:172
  186.3 2.4 copy.136
  188.6 4.2 %all-to-all-start.3 = ((bf16[2,2,98,768]{3,1,2,0:T(2,128)(2,1)}), bf16[2,2,98,768]{3,1,2,0:T(2,128)(2,1)}, u32[]{:S(2)}, u32[]{:S(2)}) async-start(bf16[2,2,98,768]{3,1,2,0:T(2,128)(2,1)} %copy.136), calls=%async_computation.3 | async-start | bytes 1204224 | tf_op jit(solution)/shard_map/all_to_all | solution.py:173
  193.2 1.5 fusion.87
  194.7 6.8 %all-to-all-done.3 = bf16[2,2,98,768]{3,1,2,0:T(2,128)(2,1)} async-done(((bf16[2,2,98,768]{3,1,2,0:T(2,128)(2,1)}), bf16[2,2,98,768]{3,1,2,0:T(2,128)(2,1)}, u32[]{:S(2)}, u32[]{:S(2)}) %all-to-all-start.3) | async-done | bytes 602144 | tf_op jit(solution)/shard_map/all_to_all | solution.py:173
  201.5 2.0 copy.137
  203.5 2.1 reshape.287
  205.6 1.9 multiply_reduce_fusion.2
  212.7 3.3 bitcast_convert_fusion.1
  216.1 3.8 %bitcast_convert_fusion = bf16[2,768,768]{1,2,0:T(8,128)(2,1)} fusion(bf16[2,2,98,768]{3,1,2,0:T(2,128)(2,1)} %all-to-all-done.2, f32[2,2,98,768]{3,2,0,1:T(8,128)} %copy-done.14), kind=kOutput, calls=%fused_computation | convolution fusion | flops 466311168 | bytes 4165632 | tf_op jit(solution)/shard_map/skcf,skcd->kfd/dot_general | solution.py:163
  222.0 2.2 reshape.295
  224.1 1.8 copy.178
  226.0 4.1 %all-to-all-start.6 = ((bf16[8,192,96]{2,1,0:T(8,128)(2,1)}), bf16[8,192,96]{2,1,0:T(8,128)(2,1)}, u32[]{:S(2)}, u32[]{:S(2)}) async-start(bf16[8,192,96]{2,1,0:T(8,128)(2,1)} %bitcast.164), calls=%async_computation.6 | async-start | bytes 786432 | tf_op jit(solution)/shard_map/all_to_all | solution.py:21
  231.6 6.3 %all-to-all-done.6 = bf16[8,192,96]{2,1,0:T(8,128)(2,1)} async-done(((bf16[8,192,96]{2,1,0:T(8,128)(2,1)}), bf16[8,192,96]{2,1,0:T(8,128)(2,1)}, u32[]{:S(2)}, u32[]{:S(2)}) %all-to-all-start.6) | async-done | bytes 294944 | tf_op jit(solution)/shard_map/all_to_all | solution.py:21
  237.8 1.7 convert_reduce_fusion.3
  239.5 8.2 %all-reduce.9.cloned.1.call-done = bf16[197,768]{1,0:T(8,128)(2,1)} async-done(((bf16[197,768]{1,0:T(8,128)(2,1)}), bf16[197,768]{1,0:T(8,128)(2,1)}) %all-reduce.9.cloned.1.call-update) | async-done | bytes 302608 | tf_op jit(solution)/shard_map/psum | solution.py:238
  247.8 2.0 fusion.56
  251.6 3.6 %all-to-all-start.4 = ((bf16[8,96,8]{1,2,0:T(8,128)(2,1)}), bf16[8,96,8]{1,2,0:T(8,128)(2,1)S(1)}, u32[]{:S(2)}, u32[]{:S(2)}) async-start(bf16[8,96,8]{1,2,0:T(8,128)(2,1)} %concatenate.12), calls=%async_computation.4 | async-start | bytes 32768 | tf_op jit(solution)/shard_map/all_to_all | solution.py:21
  255.2 1.9 copy.164
  257.1 1.4 fusion.38
  261.5 4.3 %all-to-all-start.5 = ((bf16[8,3,96,192]{3,2,1,0:T(8,128)(2,1)}), bf16[8,3,96,192]{3,2,1,0:T(8,128)(2,1)}, u32[]{:S(2)}, u32[]{:S(2)}) async-start(bf16[8,3,96,192]{3,2,1,0:T(8,128)(2,1)} %copy.150), calls=%async_computation.5 | async-start | bytes 2359296 | tf_op jit(solution)/shard_map/all_to_all | solution.py:21
  265.8 2.0 fusion.53
  269.0 19.1 %all-to-all-done.5 = bf16[8,3,96,192]{3,2,1,0:T(8,128)(2,1)} async-done(((bf16[8,3,96,192]{3,2,1,0:T(8,128)(2,1)}), bf16[8,3,96,192]{3,2,1,0:T(8,128)(2,1)}, u32[]{:S(2)}, u32[]{:S(2)}) %all-to-all-start.5) | async-done | bytes 884768 | tf_op jit(solution)/shard_map/all_to_all | solution.py:21
  288.0 2.2 convert_reduce_fusion
  290.2 5.2 %reduce-scatter.3.cloned.1.call-done = bf16[2,192,768]{2,1,0:T(8,128)(2,1)} async-done(((bf16[2,768,768]{2,1,0:T(8,128)(2,1)}), bf16[2,192,768]{2,1,0:T(8,128)(2,1)}) %reduce-scatter.3.cloned.1.call-update) | async-done | bytes 589840 | tf_op jit(solution)/shard_map/reduce_scatter | solution.py:181
  295.4 2.2 convert_element_type.252
  297.6 32.4 %reduce-scatter.5.cloned.1.call-done = bf16[2,768,192]{1,2,0:T(8,128)(2,1)} async-done(((bf16[2,768,768]{1,2,0:T(8,128)(2,1)}), bf16[2,768,192]{1,2,0:T(8,128)(2,1)}) %reduce-scatter.5.cloned.1.call-update) | async-done | bytes 589840 | tf_op jit(solution)/shard_map/reduce_scatter | solution.py:184
  330.0 2.2 convert_element_type.254
  (154 shorter events, 28.1 us)
Async XLA Ops:
  7.2 79.5 %copy-start = (bf16[2,768,768]{2,1,0:T(8,128)(2,1)S(1)}, bf16[2,768,768]{2,1,0:T(8,128)(2,1)}, u32[]{:S(2)}) copy-start(bf16[2,768,768]{2,1,0:T(8,128)(2,1)} %param.22) | copy-start | bytes 7077892
  7.2 4.1 %copy-start.6 = (bf16[197,768]{1,0:T(8,128)(2,1)S(1)}, bf16[197,768]{1,0:T(8,128)(2,1)}, u32[]{:S(2)}) copy-start(bf16[197,768]{1,0:T(8,128)(2,1)} %param.13) | copy-start | bytes 907780
  7.2 4.1 %copy-start.17 = (bf16[3,768,192]{1,2,0:T(8,128)(2,1)S(1)}, bf16[3,768,192]{1,2,0:T(8,128)(2,1)}, u32[]{:S(2)}) copy-start(bf16[3,768,192]{1,2,0:T(8,128)(2,1)} %param.16) | copy-start | bytes 2654212
  7.2 50.8 %all-reduce.5.cloned.1.call-start = ((), (), s32[]{:S(2)}) async-start(), calls=%async_computation.9 | async-start | bytes 1228800 | tf_op jit(solution)/shard_map/psum | solution.py:108
  7.3 4.0 %copy-start.34 = (f32[768]{0:T(1024)S(1)}, f32[768]{0:T(1024)}, u32[]{:S(2)}) copy-start(f32[768]{0:T(1024)} %param.14) | copy-start | bytes 9220
  7.3 4.0 %copy-start.39 = (f32[768]{0:T(1024)S(1)}, f32[768]{0:T(1024)}, u32[]{:S(2)}) copy-start(f32[768]{0:T(1024)} %param.15) | copy-start | bytes 9220
  9.7 2.0 copy-start.36
  11.3 1.3 copy-start.24
  12.1 1.4 copy-start.28
  12.1 2.1 copy-start.15
  12.6 2.7 copy-start.32
  12.6 2.7 copy-start.33
  15.3 44.1 %copy-start.31 = (f32[768]{0:T(1024)S(1)}, f32[768]{0:T(1024)}, u32[]{:S(2)}) copy-start(f32[768]{0:T(1024)} %param.18) | copy-start | bytes 9220
  15.3 44.1 %copy-start.38 = (f32[768]{0:T(1024)S(1)}, f32[768]{0:T(1024)}, u32[]{:S(2)}) copy-start(f32[768]{0:T(1024)} %param.19) | copy-start | bytes 9220
  15.5 44.2 %copy-start.30 = (f32[768,4]{0,1:T(4,128)S(1)}, f32[768,4]{0,1:T(4,128)}, u32[]{:S(2)}) copy-start(f32[768,4]{0,1:T(4,128)} %param.20) | copy-start | bytes 36868
  66.0 12.8 %all-to-all-start = ((bf16[2,2,98,768]{3,1,2,0:T(2,128)(2,1)}), bf16[2,2,98,768]{3,1,2,0:T(2,128)(2,1)}, u32[]{:S(2)}, u32[]{:S(2)}) async-start(bf16[2,2,98,768]{3,1,2,0:T(2,128)(2,1)} %copy.130), calls=%async_computation | async-start | bytes 1204224 | tf_op jit(solution)/shard_map/all_to_all | solution.py:128
  78.8 58.0 %all-to-all-start.2 = ((bf16[2,2,98,768]{3,1,2,0:T(2,128)(2,1)}), bf16[2,2,98,768]{3,1,2,0:T(2,128)(2,1)}, u32[]{:S(2)}, u32[]{:S(2)}) async-start(bf16[2,2,98,768]{3,1,2,0:T(2,128)(2,1)} %copy.134), calls=%async_computation.2 | async-start | bytes 1204224 | tf_op jit(solution)/shard_map/all_to_all | solution.py:156
  85.6 1.1 copy-start.14
  136.7 11.6 %all-to-all-start.1 = ((bf16[2,2,98,768]{3,1,2,0:T(2,128)(2,1)}), bf16[2,2,98,768]{3,1,2,0:T(2,128)(2,1)}, u32[]{:S(2)}, u32[]{:S(2)}) async-start(bf16[2,2,98,768]{3,1,2,0:T(2,128)(2,1)} %all-reduce.10), calls=%async_computation.1 | async-start | bytes 1204224 | tf_op jit(solution)/shard_map/all_to_all | solution.py:136
  141.0 45.3 %all-reduce.7.cloned.1.call-start = ((), (), s32[]{:S(2)}) async-start(), calls=%async_computation.10 | async-start | bytes 1277952 | tf_op jit(solution)/shard_map/psum | solution.py:172
  141.1 3.7 %copy-start.5 = (bf16[2,768,768]{2,1,0:T(8,128)(2,1)S(1)}, bf16[2,768,768]{2,1,0:T(8,128)(2,1)}, u32[]{:S(2)}) copy-start(bf16[2,768,768]{2,1,0:T(8,128)(2,1)} %param.21) | copy-start | bytes 7077892
  188.6 12.9 %all-to-all-start.3 = ((bf16[2,2,98,768]{3,1,2,0:T(2,128)(2,1)}), bf16[2,2,98,768]{3,1,2,0:T(2,128)(2,1)}, u32[]{:S(2)}, u32[]{:S(2)}) async-start(bf16[2,2,98,768]{3,1,2,0:T(2,128)(2,1)} %copy.136), calls=%async_computation.3 | async-start | bytes 1204224 | tf_op jit(solution)/shard_map/all_to_all | solution.py:173
  192.9 54.9 %all-reduce.9.cloned.1.call-start = ((), (), s32[]{:S(2)}) async-start(), calls=%async_computation.11 | async-start | bytes 614400 | tf_op jit(solution)/shard_map/psum | solution.py:238
  205.6 2.0 copy-start.9
  205.6 2.0 copy-start.23
  207.5 1.1 copy-start.16
  207.5 1.4 copy-start.13
  208.6 1.8 copy-start.3
  208.6 1.3 copy-start.2
  208.6 1.3 copy-start.25
  208.6 1.6 copy-start.29
  208.6 1.8 copy-start.27
  209.9 1.2 copy-start.18
  210.4 1.2 copy-start.21
  210.7 1.0 copy-start.19
  211.4 1.4 copy-start.11
  212.7 82.8 %reduce-scatter.3.cloned.1.call-start = ((), (), s32[]{:S(2)}) async-start(), calls=%async_computation.12 | async-start | bytes 2949120 | tf_op jit(solution)/shard_map/reduce_scatter | solution.py:181
  216.1 113.9 %reduce-scatter.5.cloned.1.call-start = ((), (), s32[]{:S(2)}) async-start(), calls=%async_computation.13 | async-start | bytes 2949120 | tf_op jit(solution)/shard_map/reduce_scatter | solution.py:184
  219.9 1.1 copy-start.4
  224.1 23.6 %copy-start.35 = (f32[768]{0:T(1024)S(1)}, f32[768]{0:T(1024)}, u32[]{:S(2)}) copy-start(f32[768]{0:T(1024)} %param.14) | copy-start | bytes 9220
  224.1 23.6 %copy-start.37 = (f32[197]{0:T(256)S(1)}, f32[197]{0:T(256)}, u32[]{:S(2)}) copy-start(f32[197]{0:T(256)} %copy-done.36) | copy-start | bytes 2368
  224.1 23.6 %copy-start.40 = (f32[768]{0:T(1024)S(1)}, f32[768]{0:T(1024)}, u32[]{:S(2)}) copy-start(f32[768]{0:T(1024)} %param.15) | copy-start | bytes 9220
  226.0 11.9 %all-to-all-start.6 = ((bf16[8,192,96]{2,1,0:T(8,128)(2,1)}), bf16[8,192,96]{2,1,0:T(8,128)(2,1)}, u32[]{:S(2)}, u32[]{:S(2)}) async-start(bf16[8,192,96]{2,1,0:T(8,128)(2,1)} %bitcast.164), calls=%async_computation.6 | async-start | bytes 786432 | tf_op jit(solution)/shard_map/all_to_all | solution.py:21
  239.5 18.9 %copy-start.20 = (bf16[3,64,197]{2,1,0:T(8,128)(2,1)S(1)}, bf16[3,64,197]{2,1,0:T(8,128)(2,1)}, u32[]{:S(2)}) copy-start(bf16[3,64,197]{2,1,0:T(8,128)(2,1)} %copy-done.19) | copy-start | bytes 226948
  251.6 9.9 %all-to-all-start.4 = ((bf16[8,96,8]{1,2,0:T(8,128)(2,1)}), bf16[8,96,8]{1,2,0:T(8,128)(2,1)S(1)}, u32[]{:S(2)}, u32[]{:S(2)}) async-start(bf16[8,96,8]{1,2,0:T(8,128)(2,1)} %concatenate.12), calls=%async_computation.4 | async-start | bytes 32768 | tf_op jit(solution)/shard_map/all_to_all | solution.py:21
  257.1 2.7 copy-start.7
  257.1 2.7 copy-start.22
  261.5 26.5 %all-to-all-start.5 = ((bf16[8,3,96,192]{3,2,1,0:T(8,128)(2,1)}), bf16[8,3,96,192]{3,2,1,0:T(8,128)(2,1)}, u32[]{:S(2)}, u32[]{:S(2)}) async-start(bf16[8,3,96,192]{3,2,1,0:T(8,128)(2,1)} %copy.150), calls=%async_computation.5 | async-start | bytes 2359296 | tf_op jit(solution)/shard_map/all_to_all | solution.py:21
  (5 other events, 3.9 us)
Sparse Core Ops, SparseCore 0:
  15.4 42.5 all-reduce.4
  146.6 39.5 all-reduce.6
  212.8 34.9 all-reduce.8
  250.1 45.2 reduce-scatter.2
  297.8 32.1 reduce-scatter.4
where the time goes:
time: 341 us; the launch traced here: 339 us
  waiting for transfers between devices  153 us (45%)
  blocking collectives  47.3 us (14%)
  matrix products  37.3 us (11%)
  local copies, waits for them, and re-layouts  36.2 us (11%)
  starting transfers between devices  29.3 us (9%)
  other arithmetic  21 us (6%)
  between operations  14.5 us (4%)
    psum x1, blocking collectives, per_device(): summed = lax.psum(partial_value, 'tensor')  47.3 us
    psum x1, waiting for transfers between devices, per_device(): attended = lax.psum(partial_attn, 'tensor')  42.5 us
    reduce_scatter x1, waiting for transfers between devices, per_device(): lax.psum_scatter(local_out_grad.astype(jnp.bfloat16), 'dp', scatter_dimen...  32.4 us
    psum x1, waiting for transfers between devices, per_device(): back_sum = lax.psum(partial_back.astype(jnp.bfloat16), 'tensor')  31 us
    all_to_all x3, waiting for transfers between devices, sent_and_summed(): lax.all_to_all(cut_along(shard, dim, devices), axis, 0, 0, tiled=True)  25.3 us
    all_to_all x3, starting transfers between devices, sent_and_summed(): lax.all_to_all(cut_along(shard, dim, devices), axis, 0, 0, tiled=True)  11.9 us
    psum x1, waiting for transfers between devices, per_device(): lax.psum(partial_first.astype(jnp.bfloat16), 'tensor').astype(jnp.float32)  8.2 us
    all_to_all x1, waiting for transfers between devices, per_device(): lax.all_to_all(back_sum, 'expert', split_axis=0, concat_axis=0, tiled=True)  6.82 us
  transfers between devices with their start and end apart: 12, of which 9 were waited for; matrix products, arithmetic and copies ran while one was open for 18% of the time, Pallas kernels for 0%

commit v1 on v0

--- a/solution.py
+++ b/solution.py
@@ -169,7 +169,7 @@
     partial_back = jnp.einsum(
         "skcf,kdf->skcd", pre_grad, expert_in, preferred_element_type=jnp.float32
     )
-    back_sum = lax.psum(partial_back.astype(jnp.bfloat16), "tensor")
+    back_sum = jnp.sum(lax.all_gather(partial_back.astype(jnp.bfloat16), "tensor"), axis=0)
     back_home = lax.all_to_all(back_sum, "expert", split_axis=0, concat_axis=0, tiled=True)
     back_rows = jnp.einsum(
         "rjq,qd->rd",

time: 341 us -> 365 us (1.070)
  blocking collectives: 47.3 us -> 86.1 us
  waiting for transfers between devices: 153 us -> 132 us
  matrix products: 37.3 us -> 41.2 us
    psum x1, blocking collectives: 47.3 us -> 86.1 us  [per_device(): summed = lax.psum(partial_value, 'tensor')]
    psum x1 -> x0, waiting for transfers between devices: 31 us -> none  [per_device(): back_sum = lax.psum(partial_back.astype(jnp.bfloat16), 'tensor')]
    reduce_scatter x1, waiting for transfers between devices: 5.22 us -> 26.5 us  [per_device(): lax.psum_scatter(local_in_grad.astype(jnp.bfloat16), 'dp', scatter_dimens...]
    all_to_all x3, waiting for transfers between devices: 25.3 us -> 6.45 us  [sent_and_summed(): lax.all_to_all(cut_along(shard, dim, devices), axis, 0, 0, tiled=True)]
    all_to_all x1, waiting for transfers between devices: 0.01 us -> 5.6 us  [per_device(): lax.all_to_all(grad_send, 'expert', split_axis=0, concat_axis=0, tiled=True)]
    all_to_all x1, waiting for transfers between devices: 0.01 us -> 5.43 us  [per_device(): lax.all_to_all(summed.astype(jnp.bfloat16), 'expert', split_axis=0, conca...]
  transfers between devices with their start and end apart: 12 -> 12, of which waited for: 9 -> 10; matrix products, arithmetic and copies ran while one was open for 18% -> 16% of each run, Pallas kernels for 0% -> 0%
where the time goes in v1:
time: 365 us; the launch traced here: 363 us
  waiting for transfers between devices  132 us (36%)
  blocking collectives  86.1 us (24%)
  matrix products  41.2 us (11%)
  local copies, waits for them, and re-layouts  35.9 us (10%)
  starting transfers between devices  29.3 us (8%)
  other arithmetic  24.1 us (7%)
  between operations  14.5 us (4%)
    psum x1, blocking collectives, per_device(): summed = lax.psum(partial_value, 'tensor')  86.1 us
    psum x1, waiting for transfers between devices, per_device(): attended = lax.psum(partial_attn, 'tensor')  42.5 us
    reduce_scatter x1, waiting for transfers between devices, per_device(): lax.psum_scatter(local_out_grad.astype(jnp.bfloat16), 'dp', scatter_dimen...  32.3 us
    reduce_scatter x1, waiting for transfers between devices, per_device(): lax.psum_scatter(local_in_grad.astype(jnp.bfloat16), 'dp', scatter_dimens...  26.5 us
    all_to_all x3, starting transfers between devices, sent_and_summed(): lax.all_to_all(cut_along(shard, dim, devices), axis, 0, 0, tiled=True)  11.9 us
    psum x1, waiting for transfers between devices, per_device(): lax.psum(partial_first.astype(jnp.bfloat16), 'tensor').astype(jnp.float32)  7.69 us
  transfers between devices with their start and end apart: 12, of which 10 were waited for; matrix products, arithmetic and copies ran while one was open for 16% of the time, Pallas kernels for 0%

profile of v1, /device:TPU:0, one launch (start us, length us, event | category | flops | bytes accessed | tf_op | source)
XLA Modules:
  0.0 363.1 jit_solution(13094152830921790469)
XLA Ops:
  9.8 1.5 convolution_convert_fusion.11
  15.5 42.5 %all-reduce.4.cloned.1.call-done = f32[197,768]{1,0:T(8,128)} async-done(((f32[197,768]{1,0:T(8,128)}), f32[197,768]{1,0:T(8,128)}) %all-reduce.4.cloned.1.call-update) | async-done | bytes 605200 | tf_op jit(solution)/shard_map/psum | solution.py:108
  61.5 2.1 reshape.284
  63.6 2.4 copy.129
  65.9 4.2 %all-to-all-start = ((bf16[2,2,98,768]{3,1,2,0:T(2,128)(2,1)}), bf16[2,2,98,768]{3,1,2,0:T(2,128)(2,1)}, u32[]{:S(2)}, u32[]{:S(2)}) async-start(bf16[2,2,98,768]{3,1,2,0:T(2,128)(2,1)} %copy.129), calls=%async_computation | async-start | bytes 1204224 | tf_op jit(solution)/shard_map/all_to_all | solution.py:128
  72.1 2.1 fusion.23
  74.2 2.1 reshape.286
  76.3 2.4 copy.133
  78.7 4.2 %all-to-all-start.2 = ((bf16[2,2,98,768]{3,1,2,0:T(2,128)(2,1)}), bf16[2,2,98,768]{3,1,2,0:T(2,128)(2,1)}, u32[]{:S(2)}, u32[]{:S(2)}) async-start(bf16[2,2,98,768]{3,1,2,0:T(2,128)(2,1)} %copy.133), calls=%async_computation.2 | async-start | bytes 1204224 | tf_op jit(solution)/shard_map/all_to_all | solution.py:156
  83.0 2.8 fusion.14
  85.8 5.6 %all-to-all-done.2 = bf16[2,2,98,768]{3,1,2,0:T(2,128)(2,1)} async-done(((bf16[2,2,98,768]{3,1,2,0:T(2,128)(2,1)}), bf16[2,2,98,768]{3,1,2,0:T(2,128)(2,1)}, u32[]{:S(2)}, u32[]{:S(2)}) %all-to-all-start.2) | async-done | bytes 602144 | tf_op jit(solution)/shard_map/all_to_all | solution.py:156
  91.4 3.4 fusion.17
  95.7 1.7 fusion.29
  97.5 2.8 fusion.6
  100.3 2.0 copy.176
  102.3 86.1 %all-reduce.7 = bf16[2,2,98,768]{3,1,2,0:T(2,128)(2,1)} all-reduce(f32[2,2,98,768]{3,1,2,0:T(2,128)} %bitcast.164), channel_id=1, replica_groups=mesh['dp'=4,'expert'=2,'tensor'=4] {'tensor'}, use_global_device_ids=true, to_apply=%region_11.12 | all-reduce | flops 301056 | bytes 1806336 | tf_op jit(solution)/shard_map/psum | solution.py:135
  188.4 4.4 %all-to-all-start.1 = ((bf16[2,2,98,768]{3,1,2,0:T(2,128)(2,1)}), bf16[2,2,98,768]{3,1,2,0:T(2,128)(2,1)}, u32[]{:S(2)}, u32[]{:S(2)}) async-start(bf16[2,2,98,768]{3,1,2,0:T(2,128)(2,1)} %all-reduce.7), calls=%async_computation.1 | async-start | bytes 1204224 | tf_op jit(solution)/shard_map/all_to_all | solution.py:136
  192.8 1.8 convert_element_type.220
  194.6 5.4 %all-to-all-done.1 = bf16[2,2,98,768]{3,1,2,0:T(2,128)(2,1)} async-done(((bf16[2,2,98,768]{3,1,2,0:T(2,128)(2,1)}), bf16[2,2,98,768]{3,1,2,0:T(2,128)(2,1)}, u32[]{:S(2)}, u32[]{:S(2)}) %all-to-all-start.1) | async-done | bytes 602144 | tf_op jit(solution)/shard_map/all_to_all | solution.py:136
  200.1 2.0 copy.132
  202.0 2.1 reshape.302
  204.1 2.8 multiply_reduce_fusion
  207.0 3.1 reduce_sum.246
  210.1 2.4 copy.135
  212.5 4.2 %all-to-all-start.3 = ((bf16[2,2,98,768]{3,1,2,0:T(2,128)(2,1)}), bf16[2,2,98,768]{3,1,2,0:T(2,128)(2,1)}, u32[]{:S(2)}, u32[]{:S(2)}) async-start(bf16[2,2,98,768]{3,1,2,0:T(2,128)(2,1)} %copy.135), calls=%async_computation.3 | async-start | bytes 1204224 | tf_op jit(solution)/shard_map/all_to_all | solution.py:173
  216.8 1.5 fusion.87
  218.3 5.5 %all-to-all-done.3 = bf16[2,2,98,768]{3,1,2,0:T(2,128)(2,1)} async-done(((bf16[2,2,98,768]{3,1,2,0:T(2,128)(2,1)}), bf16[2,2,98,768]{3,1,2,0:T(2,128)(2,1)}, u32[]{:S(2)}, u32[]{:S(2)}) %all-to-all-start.3) | async-done | bytes 602144 | tf_op jit(solution)/shard_map/all_to_all | solution.py:173
  223.8 2.0 copy.136
  225.8 2.1 reshape.287
  227.8 1.9 multiply_reduce_fusion.2
  235.3 3.3 bitcast_convert_fusion.1
  238.7 3.8 %bitcast_convert_fusion = bf16[2,768,768]{1,2,0:T(8,128)(2,1)} fusion(bf16[2,2,98,768]{3,1,2,0:T(2,128)(2,1)} %all-to-all-done.2, f32[2,2,98,768]{3,2,0,1:T(8,128)} %fusion.14), kind=kOutput, calls=%fused_computation | convolution fusion | flops 466311168 | bytes 4165632 | tf_op jit(solution)/shard_map/skcf,skcd->kfd/dot_general | solution.py:163
  244.5 2.2 reshape.295
  246.7 1.8 copy.177
  248.5 4.1 %all-to-all-start.6 = ((bf16[8,192,96]{2,1,0:T(8,128)(2,1)}), bf16[8,192,96]{2,1,0:T(8,128)(2,1)}, u32[]{:S(2)}, u32[]{:S(2)}) async-start(bf16[8,192,96]{2,1,0:T(8,128)(2,1)} %bitcast.166), calls=%async_computation.6 | async-start | bytes 786432 | tf_op jit(solution)/shard_map/all_to_all | solution.py:21
  254.1 6.3 %all-to-all-done.6 = bf16[8,192,96]{2,1,0:T(8,128)(2,1)} async-done(((bf16[8,192,96]{2,1,0:T(8,128)(2,1)}), bf16[8,192,96]{2,1,0:T(8,128)(2,1)}, u32[]{:S(2)}, u32[]{:S(2)}) %all-to-all-start.6) | async-done | bytes 294944 | tf_op jit(solution)/shard_map/all_to_all | solution.py:21
  260.4 1.7 convert_reduce_fusion.3
  262.1 7.7 %all-reduce.6.cloned.1.call-done = bf16[197,768]{1,0:T(8,128)(2,1)} async-done(((bf16[197,768]{1,0:T(8,128)(2,1)}), bf16[197,768]{1,0:T(8,128)(2,1)}) %all-reduce.6.cloned.1.call-update) | async-done | bytes 302608 | tf_op jit(solution)/shard_map/psum | solution.py:238
  269.8 2.0 fusion.56
  271.8 1.9 copy.163
  275.5 3.6 all-to-all-start.4
  283.8 4.3 %all-to-all-start.5 = ((bf16[8,3,96,192]{3,2,1,0:T(8,128)(2,1)}), bf16[8,3,96,192]{3,2,1,0:T(8,128)(2,1)}, u32[]{:S(2)}, u32[]{:S(2)}) async-start(bf16[8,3,96,192]{3,2,1,0:T(8,128)(2,1)} %copy.149), calls=%async_computation.5 | async-start | bytes 2359296 | tf_op jit(solution)/shard_map/all_to_all | solution.py:21
  288.1 2.1 fusion.53
  291.3 26.5 %reduce-scatter.3.cloned.1.call-done = bf16[2,192,768]{2,1,0:T(8,128)(2,1)} async-done(((bf16[2,768,768]{2,1,0:T(8,128)(2,1)}), bf16[2,192,768]{2,1,0:T(8,128)(2,1)}) %reduce-scatter.3.cloned.1.call-update) | async-done | bytes 589840 | tf_op jit(solution)/shard_map/reduce_scatter | solution.py:181
  317.7 2.2 convert_element_type.254
  319.9 32.3 %reduce-scatter.5.cloned.1.call-done = bf16[2,768,192]{1,2,0:T(8,128)(2,1)} async-done(((bf16[2,768,768]{1,2,0:T(8,128)(2,1)}), bf16[2,768,192]{1,2,0:T(8,128)(2,1)}) %reduce-scatter.5.cloned.1.call-update) | async-done | bytes 589840 | tf_op jit(solution)/shard_map/reduce_scatter | solution.py:184
  352.2 2.2 convert_element_type.256
  354.4 2.2 convert_reduce_fusion
  (149 shorter events, 29.5 us)
Async XLA Ops:
  7.2 75.8 %copy-start = (bf16[2,768,768]{2,1,0:T(8,128)(2,1)S(1)}, bf16[2,768,768]{2,1,0:T(8,128)(2,1)}, u32[]{:S(2)}) copy-start(bf16[2,768,768]{2,1,0:T(8,128)(2,1)} %param.21) | copy-start | bytes 7077892
  7.2 4.1 %copy-start.5 = (bf16[197,768]{1,0:T(8,128)(2,1)S(1)}, bf16[197,768]{1,0:T(8,128)(2,1)}, u32[]{:S(2)}) copy-start(bf16[197,768]{1,0:T(8,128)(2,1)} %param.13) | copy-start | bytes 907780
  7.2 4.1 %copy-start.15 = (bf16[3,768,192]{1,2,0:T(8,128)(2,1)S(1)}, bf16[3,768,192]{1,2,0:T(8,128)(2,1)}, u32[]{:S(2)}) copy-start(bf16[3,768,192]{1,2,0:T(8,128)(2,1)} %param.16) | copy-start | bytes 2654212
  7.2 50.8 %all-reduce.4.cloned.1.call-start = ((), (), s32[]{:S(2)}) async-start(), calls=%async_computation.9 | async-start | bytes 1228800 | tf_op jit(solution)/shard_map/psum | solution.py:108
  7.3 4.0 %copy-start.31 = (f32[768]{0:T(1024)S(1)}, f32[768]{0:T(1024)}, u32[]{:S(2)}) copy-start(f32[768]{0:T(1024)} %param.14) | copy-start | bytes 9220
  7.3 4.0 %copy-start.36 = (f32[768]{0:T(1024)S(1)}, f32[768]{0:T(1024)}, u32[]{:S(2)}) copy-start(f32[768]{0:T(1024)} %param.15) | copy-start | bytes 9220
  9.7 2.0 copy-start.33
  11.3 0.9 copy-start.23
  11.7 0.9 copy-start.25
  12.1 1.4 copy-start.21
  12.1 2.0 copy-start.13
  12.5 0.8 copy-start.1
  12.6 2.7 copy-start.29
  12.6 2.7 copy-start.30
  15.3 44.1 %copy-start.28 = (f32[768]{0:T(1024)S(1)}, f32[768]{0:T(1024)}, u32[]{:S(2)}) copy-start(f32[768]{0:T(1024)} %param.18) | copy-start | bytes 9220
  15.3 44.1 %copy-start.35 = (f32[768]{0:T(1024)S(1)}, f32[768]{0:T(1024)}, u32[]{:S(2)}) copy-start(f32[768]{0:T(1024)} %param.19) | copy-start | bytes 9220
  63.5 6.6 %copy-start.27 = (f32[768,4]{0,1:T(4,128)S(1)}, f32[768,4]{0,1:T(4,128)}, u32[]{:S(2)}) copy-start(f32[768,4]{0,1:T(4,128)} %param.20) | copy-start | bytes 36868
  65.9 12.8 %all-to-all-start = ((bf16[2,2,98,768]{3,1,2,0:T(2,128)(2,1)}), bf16[2,2,98,768]{3,1,2,0:T(2,128)(2,1)}, u32[]{:S(2)}, u32[]{:S(2)}) async-start(bf16[2,2,98,768]{3,1,2,0:T(2,128)(2,1)} %copy.129), calls=%async_computation | async-start | bytes 1204224 | tf_op jit(solution)/shard_map/all_to_all | solution.py:128
  78.7 12.7 %all-to-all-start.2 = ((bf16[2,2,98,768]{3,1,2,0:T(2,128)(2,1)}), bf16[2,2,98,768]{3,1,2,0:T(2,128)(2,1)}, u32[]{:S(2)}, u32[]{:S(2)}) async-start(bf16[2,2,98,768]{3,1,2,0:T(2,128)(2,1)} %copy.133), calls=%async_computation.2 | async-start | bytes 1204224 | tf_op jit(solution)/shard_map/all_to_all | solution.py:156
  83.0 124.0 %all-gather.3.cloned.1.call-start = ((), (), s32[]{:S(2)}) async-start(), calls=%async_computation.13 | async-start | bytes 3194880 | tf_op jit(solution)/shard_map/all_gather | solution.py:172
  94.9 0.8 copy-start.9
  188.4 11.7 %all-to-all-start.1 = ((bf16[2,2,98,768]{3,1,2,0:T(2,128)(2,1)}), bf16[2,2,98,768]{3,1,2,0:T(2,128)(2,1)}, u32[]{:S(2)}, u32[]{:S(2)}) async-start(bf16[2,2,98,768]{3,1,2,0:T(2,128)(2,1)} %all-reduce.7), calls=%async_computation.1 | async-start | bytes 1204224 | tf_op jit(solution)/shard_map/all_to_all | solution.py:136
  212.5 11.3 %all-to-all-start.3 = ((bf16[2,2,98,768]{3,1,2,0:T(2,128)(2,1)}), bf16[2,2,98,768]{3,1,2,0:T(2,128)(2,1)}, u32[]{:S(2)}, u32[]{:S(2)}) async-start(bf16[2,2,98,768]{3,1,2,0:T(2,128)(2,1)} %copy.135), calls=%async_computation.3 | async-start | bytes 1204224 | tf_op jit(solution)/shard_map/all_to_all | solution.py:173
  216.7 53.1 %all-reduce.6.cloned.1.call-start = ((), (), s32[]{:S(2)}) async-start(), calls=%async_computation.10 | async-start | bytes 614400 | tf_op jit(solution)/shard_map/psum | solution.py:238
  227.8 2.0 copy-start.8
  227.8 2.0 copy-start.20
  229.8 1.1 copy-start.14
  230.9 1.9 copy-start.3
  230.9 1.3 copy-start.2
  230.9 1.6 copy-start.12
  230.9 1.6 copy-start.22
  231.2 1.7 copy-start.26
  232.2 0.9 copy-start.24
  232.4 1.2 copy-start.16
  233.1 0.8 copy-start.19
  233.3 0.9 copy-start.17
  233.9 1.4 copy-start.10
  235.2 82.5 %reduce-scatter.3.cloned.1.call-start = ((), (), s32[]{:S(2)}) async-start(), calls=%async_computation.11 | async-start | bytes 2949120 | tf_op jit(solution)/shard_map/reduce_scatter | solution.py:181
  238.6 113.6 %reduce-scatter.5.cloned.1.call-start = ((), (), s32[]{:S(2)}) async-start(), calls=%async_computation.12 | async-start | bytes 2949120 | tf_op jit(solution)/shard_map/reduce_scatter | solution.py:184
  242.5 1.1 copy-start.4
  246.7 23.1 %copy-start.32 = (f32[768]{0:T(1024)S(1)}, f32[768]{0:T(1024)}, u32[]{:S(2)}) copy-start(f32[768]{0:T(1024)} %param.14) | copy-start | bytes 9220
  246.7 23.1 %copy-start.34 = (f32[197]{0:T(256)S(1)}, f32[197]{0:T(256)}, u32[]{:S(2)}) copy-start(f32[197]{0:T(256)} %copy-done.33) | copy-start | bytes 2368
  246.7 23.1 %copy-start.37 = (f32[768]{0:T(1024)S(1)}, f32[768]{0:T(1024)}, u32[]{:S(2)}) copy-start(f32[768]{0:T(1024)} %param.15) | copy-start | bytes 9220
  248.5 11.9 %all-to-all-start.6 = ((bf16[8,192,96]{2,1,0:T(8,128)(2,1)}), bf16[8,192,96]{2,1,0:T(8,128)(2,1)}, u32[]{:S(2)}, u32[]{:S(2)}) async-start(bf16[8,192,96]{2,1,0:T(8,128)(2,1)} %bitcast.166), calls=%async_computation.6 | async-start | bytes 786432 | tf_op jit(solution)/shard_map/all_to_all | solution.py:21
  262.1 18.4 %copy-start.18 = (bf16[3,64,197]{2,1,0:T(8,128)(2,1)S(1)}, bf16[3,64,197]{2,1,0:T(8,128)(2,1)}, u32[]{:S(2)}) copy-start(bf16[3,64,197]{2,1,0:T(8,128)(2,1)} %copy-done.17) | copy-start | bytes 226948
  275.5 8.3 %all-to-all-start.4 = ((bf16[8,96,8]{1,2,0:T(8,128)(2,1)}), bf16[8,96,8]{1,2,0:T(8,128)(2,1)S(1)}, u32[]{:S(2)}, u32[]{:S(2)}) async-start(bf16[8,96,8]{1,2,0:T(8,128)(2,1)} %concatenate.12), calls=%async_computation.4 | async-start | bytes 32768 | tf_op jit(solution)/shard_map/all_to_all | solution.py:21
  279.1 2.7 copy-start.6
  283.8 70.6 %all-to-all-start.5 = ((bf16[8,3,96,192]{3,2,1,0:T(8,128)(2,1)}), bf16[8,3,96,192]{3,2,1,0:T(8,128)(2,1)}, u32[]{:S(2)}, u32[]{:S(2)}) async-start(bf16[8,3,96,192]{3,2,1,0:T(8,128)(2,1)} %copy.149), calls=%async_computation.5 | async-start | bytes 2359296 | tf_op jit(solution)/shard_map/all_to_all | solution.py:21
  (2 other events, 1.3 us)
Sparse Core Ops, SparseCore 0:
  15.4 42.5 all-reduce.3
  97.6 88.5 all-gather.2
  235.3 34.4 all-reduce.5
  272.2 45.5 reduce-scatter.2
  320.1 32.0 reduce-scatter.4
